TPU v7x, 128 devices: a whole 4x4x4 slice. The times are simulated.
128 devices in a mesh: row: 16 (over y, z), col: 8 (over x, core).
Axes of the slice: x: 4, y: 4, z: 4, core: 2. Of those that a mesh axis runs over, the one named last changes fastest.
Arguments:
- descriptors: bfloat16 [131072, 512], P(('row', 'col')), may hold values from -6 to 6
- center_index: int32 [16384], replicated, may hold values from 0 to 131071, as said below
- panel_index: int32 [1], replicated, may hold values from 0 to 15
Outputs:
- schur: float32 [16384, 16384], P('row', 'col')
- panel_factor: float32 [16384, 1024], P('row', 'col')
Inputs may be any that keep to these rules, and one draw needn't show every extreme that they name: Center j is row center_index[j] mod 1024 of shard center_index[j] // 1024, shards numbered row-major over row and col. In each aligned run of 128 centers no shard supplies more than 4 centers, and some shard supplies exactly 4.
All inputs are finite; a program needn't handle non-finite values.
Results may differ from a plain program's by a relative error of at most 0.0003.
Values may be sent and summed in bfloat16 or wider, within the bound.
No kernel may reach another device: no remote copies, remote signals or barrier semaphores. Data moves between devices by JAX's collectives and lax.ppermute only.
A program may use at most 128 MiB of HBM per device.

v0:
```python
import jax
import jax.numpy as jnp
from jax import lax
from jax.sharding import PartitionSpec as P

D = 512
PANEL = 1024
GROUP = 128
ridge = 1.0


def broadcast(block, axis, holder):
    block = jnp.where(lax.axis_index(axis) == holder, block, jnp.zeros_like(block))
    return lax.psum(block, axis)


def gram_block(left, right, left_sq, right_sq):
    inner = lax.dot_general(
        left, right, (((1,), (1,)), ((), ())), preferred_element_type=jnp.float32
    )
    return jnp.exp(-(left_sq[:, None] + right_sq[None, :] - 2.0 * inner) / D)


def squares(values):
    return jnp.sum(jnp.square(values.astype(jnp.float32)), axis=1)


def transposed_product(left, right):
    return lax.dot_general(
        left,
        right,
        (((1,), (1,)), ((), ())),
        precision=lax.Precision.HIGHEST,
        preferred_element_type=jnp.float32,
    )


def body(descriptors, center_index, panel_index):
    rows_axis = lax.axis_size("row")
    cols_axis = lax.axis_size("col")
    device_count = rows_axis * cols_axis
    my_row = lax.axis_index("row")
    my_col = lax.axis_index("col")
    my_flat = my_row * cols_axis + my_col
    data_rows = descriptors.shape[0]
    capacity = max(4, 2 * GROUP // device_count)
    tile_rows = GROUP * cols_axis
    by_group = center_index.reshape(device_count, GROUP)
    shard_of = by_group // data_rows
    same_shard = shard_of[:, :, None] == shard_of[:, None, :]
    earlier = (
        jnp.arange(GROUP, dtype=jnp.int32)[None, :] < jnp.arange(GROUP, dtype=jnp.int32)[:, None]
    )
    slot_rank = jnp.sum((same_shard & earlier[None, :, :]).astype(jnp.int32), axis=2)
    targets = jnp.where(
        shard_of == my_flat,
        jnp.arange(device_count, dtype=jnp.int32)[:, None] * capacity + slot_rank,
        device_count * capacity,
    )
    local_row = by_group - my_flat * data_rows
    slot_rows = (
        jnp.zeros((device_count * capacity,), jnp.int32)
        .at[targets.reshape(-1)]
        .set(local_row.reshape(-1), mode="drop")
    )
    outgoing = jnp.take(descriptors, slot_rows, axis=0)
    arrived = lax.all_to_all(
        outgoing.reshape(device_count, capacity, D),
        ("row", "col"),
        split_axis=0,
        concat_axis=0,
        tiled=True,
    )
    my_shards = lax.dynamic_index_in_dim(shard_of, my_flat, 0, keepdims=False)
    my_ranks = lax.dynamic_index_in_dim(slot_rank, my_flat, 0, keepdims=False)
    my_centers = arrived[my_shards, my_ranks]
    row_centers = lax.all_gather(my_centers, "col", axis=0, tiled=True)
    col_centers = lax.all_gather(my_centers, "row", axis=0, tiled=True)
    row_sq = squares(row_centers)
    col_sq = squares(col_centers)
    row_pos = my_row * tile_rows + jnp.arange(tile_rows, dtype=jnp.int32)
    col_pos = (
        (jnp.arange(rows_axis, dtype=jnp.int32)[:, None] * cols_axis + my_col) * GROUP
        + jnp.arange(GROUP, dtype=jnp.int32)[None, :]
    ).reshape(-1)
    tile = gram_block(row_centers, col_centers, row_sq, col_sq)
    tile = tile + ridge * (row_pos[:, None] == col_pos[None, :]).astype(jnp.float32)
    start_pos = panel_index[0] * PANEL
    first_pos = start_pos + 0
    owner_row = first_pos // tile_rows
    pieces = broadcast(row_centers, "row", owner_row)
    panel_sq = squares(pieces)
    panel_pos = start_pos + jnp.arange(PANEL, dtype=jnp.int32)
    diag_block = gram_block(pieces, pieces, panel_sq, panel_sq) + ridge * jnp.eye(
        PANEL, dtype=jnp.float32
    )
    diag_factor = jnp.linalg.cholesky(diag_block)
    row_block = gram_block(row_centers, pieces, row_sq, panel_sq)
    row_block = row_block + ridge * (row_pos[:, None] == panel_pos[None, :]).astype(jnp.float32)
    row_factor = lax.linalg.triangular_solve(
        diag_factor, row_block, left_side=False, lower=True, transpose_a=True
    )
    own_rows = lax.dynamic_slice_in_dim(row_factor, my_col * GROUP, GROUP, 0)
    schur = tile - transposed_product(
        row_factor, lax.all_gather(own_rows, "row", axis=0, tiled=True)
    )
    share = PANEL // cols_axis
    panel_factor = lax.dynamic_slice_in_dim(row_factor, my_col * share, share, 1)
    return (schur, panel_factor)


def solution(mesh):
    return jax.shard_map(
        body,
        mesh=mesh,
        in_specs=(P(("row", "col"), None), P(), P()),
        out_specs=(P("row", "col"), P("row", "col")),
        check_vma=False,
    )
```

profile of v0, /device:TPU:0, one launch (start us, length us, event | category | flops | bytes accessed | tf_op | source)
XLA Modules:
  0.0 700.6 jit_solution(14249034032198965943)
XLA Ops:
  8.2 5.1 convert_reduce_fusion
  14.3 60.3 %scatter_custom_fusion = s32[512]{0:T(512)S(1)} fusion(s32[16384]{0:T(1024)S(1)} %get-tuple-element.74, s32[16384]{0:T(1024)S(1)} %get-tuple-element.73, s32[]{:T(128)} %copy.83), kind=kCustom, calls=%fused_computation.197 | custom fusion | bytes 2052 | tf_op jit(solution)/shard_map/scatter | solution.py:64
  74.6 2.0 gather_fusion
  78.0 11.2 %all-to-all-start = ((bf16[128,4,512]{2,1,0:T(4,128)(2,1)}), bf16[128,4,512]{2,1,0:T(4,128)(2,1)S(1)}, u32[]{:S(2)}, u32[]{:S(2)}) async-start(bf16[128,4,512]{2,1,0:T(4,128)(2,1)} %broadcast_select_fusion.1), calls=%async_computation | async-start | bytes 1048576 | tf_op jit(solution)/shard_map/all_to_all | solution.py:67
  89.2 13.4 %all-to-all-done = bf16[128,4,512]{2,1,0:T(4,128)(2,1)S(1)} async-done(((bf16[128,4,512]{2,1,0:T(4,128)(2,1)}), bf16[128,4,512]{2,1,0:T(4,128)(2,1)S(1)}, u32[]{:S(2)}, u32[]{:S(2)}) %all-to-all-start) | async-done | bytes 524320 | tf_op jit(solution)/shard_map/all_to_all | solution.py:67
  102.7 2.0 gather_fusion.1
  105.4 18.7 %all-gather.4.cloned.1.call-done = bf16[1024,512]{1,0:T(8,128)(2,1)} async-done(((bf16[128,512]{1,0:T(8,128)(2,1)}), bf16[1024,512]{1,0:T(8,128)(2,1)}) %all-gather.4.cloned.1.call-update) | async-done | bytes 1048592 | tf_op jit(solution)/shard_map/all_gather | solution.py:77
  125.9 1.5 multiply_reduce_fusion.2
  127.4 87.8 %all-reduce.3.cloned.1.call-done = bf16[1024,512]{1,0:T(8,128)(2,1)} async-done(((bf16[1024,512]{1,0:T(8,128)(2,1)}), bf16[1024,512]{1,0:T(8,128)(2,1)}) %all-reduce.3.cloned.1.call-update) | async-done | bytes 1048592 | tf_op jit(solution)/shard_map/psum | solution.py:14
  215.2 1.5 multiply_reduce_fusion.1
  216.7 7.7 %broadcast_add_fusion = (f32[1024,1024]{0,1:T(8,128)}, f32[1024,1024]{0,1:T(8,128)}, f32[1024,1024]{1,0:T(8,128)}) fusion(f32[1024]{0:T(1024)S(1)} %multiply_reduce_fusion.1, bf16[1024,512]{1,0:T(8,128)(2,1)} %all-reduce.3.cloned.1.call-done), kind=kOutput, calls=%fused_computation.24 | convolution fusion | flops 1077936128 | bytes 13635584 | tf_op jit(solution)/shard_map/dot_general | solution.py:18
  224.4 5.4 copy.20
  229.8 5.4 copy.21
  235.1 6.0 add_multiply_fusion
  241.2 1.9 copy-done.2
  243.1 11.7 %cholesky.223 = f32[128,128]{1,0:T(8,128)S(1)} custom-call(f32[128,128]{1,0:T(8,128)S(1)} %cholesky.580), custom_call_target="Cholesky" | custom-call | tf_op jit(solution)/shard_map/jit(cholesky)/cholesky | solution.py:97
  254.9 2.5 cholesky.255
  257.4 9.8 %custom-call.62 = f32[1,128,128]{1,2,0:T(8,128)S(1)} custom-call(f32[1,128,128]{2,1,0:T(8,128)S(1)} %get-tuple-element.72), custom_call_target="InvertDiagBlocksLowerTriangular" | custom-call | tf_op jit(solution)/shard_map/jit(cholesky)/cholesky | solution.py:97
  267.2 2.3 constant_dynamic-update-slice_fusion.25
  269.5 1.5 convolution_subtract_fusion.5
  271.1 11.7 %cholesky.244 = f32[128,128]{1,0:T(8,128)S(1)} custom-call(f32[128,128]{1,0:T(8,128)S(1)} %cholesky.584), custom_call_target="Cholesky" | custom-call | tf_op jit(solution)/shard_map/jit(cholesky)/cholesky | solution.py:97
  283.4 10.0 %custom-call.63 = f32[1,128,128]{1,2,0:T(8,128)S(1)} custom-call(f32[1,128,128]{2,1,0:T(8,128)S(1)} %get-tuple-element.69), custom_call_target="InvertDiagBlocksLowerTriangular" | custom-call | tf_op jit(solution)/shard_map/jit(cholesky)/cholesky | solution.py:97
  293.4 1.2 convolution_dynamic-update-slice_fusion.1
  294.6 2.1 convolution_subtract_fusion.6
  296.7 11.7 %cholesky.468 = f32[128,128]{1,0:T(8,128)S(1)} custom-call(f32[128,128]{1,0:T(8,128)S(1)} %cholesky.589), custom_call_target="Cholesky" | custom-call | tf_op jit(solution)/shard_map/jit(cholesky)/cholesky | solution.py:97
  309.7 9.8 %custom-call.64 = f32[1,128,128]{1,2,0:T(8,128)S(1)} custom-call(f32[1,128,128]{2,1,0:T(8,128)S(1)} %get-tuple-element.66), custom_call_target="InvertDiagBlocksLowerTriangular" | custom-call | tf_op jit(solution)/shard_map/jit(cholesky)/cholesky | solution.py:97
  320.7 2.3 convolution_subtract_fusion.7
  323.1 12.1 %cholesky.487 = f32[128,128]{1,0:T(8,128)S(1)} custom-call(f32[128,128]{1,0:T(8,128)S(1)} %cholesky.594), custom_call_target="Cholesky" | custom-call | tf_op jit(solution)/shard_map/jit(cholesky)/cholesky | solution.py:97
  336.5 9.8 %custom-call.65 = f32[1,128,128]{1,2,0:T(8,128)S(1)} custom-call(f32[1,128,128]{2,1,0:T(8,128)S(1)} %get-tuple-element.63), custom_call_target="InvertDiagBlocksLowerTriangular" | custom-call | tf_op jit(solution)/shard_map/jit(cholesky)/cholesky | solution.py:97
  347.3 2.3 convolution_subtract_fusion.8
  349.7 11.7 %cholesky.506 = f32[128,128]{1,0:T(8,128)S(1)} custom-call(f32[128,128]{1,0:T(8,128)S(1)} %cholesky.599), custom_call_target="Cholesky" | custom-call | tf_op jit(solution)/shard_map/jit(cholesky)/cholesky | solution.py:97
  362.8 9.8 %custom-call.66 = f32[1,128,128]{1,2,0:T(8,128)S(1)} custom-call(f32[1,128,128]{2,1,0:T(8,128)S(1)} %get-tuple-element.60), custom_call_target="InvertDiagBlocksLowerTriangular" | custom-call | tf_op jit(solution)/shard_map/jit(cholesky)/cholesky | solution.py:97
  373.6 2.5 convolution_subtract_fusion.9
  376.1 11.7 %cholesky.526 = f32[128,128]{1,0:T(8,128)S(1)} custom-call(f32[128,128]{1,0:T(8,128)S(1)} %cholesky.604), custom_call_target="Cholesky" | custom-call | tf_op jit(solution)/shard_map/jit(cholesky)/cholesky | solution.py:97
  389.0 9.8 %custom-call.67 = f32[1,128,128]{1,2,0:T(8,128)S(1)} custom-call(f32[1,128,128]{2,1,0:T(8,128)S(1)} %get-tuple-element.57), custom_call_target="InvertDiagBlocksLowerTriangular" | custom-call | tf_op jit(solution)/shard_map/jit(cholesky)/cholesky | solution.py:97
  399.8 2.2 convolution_subtract_fusion.10
  401.9 11.7 %cholesky.546 = f32[128,128]{1,0:T(8,128)S(1)} custom-call(f32[128,128]{1,0:T(8,128)S(1)} %cholesky.609), custom_call_target="Cholesky" | custom-call | tf_op jit(solution)/shard_map/jit(cholesky)/cholesky | solution.py:97
  414.9 10.0 %custom-call.68 = f32[1,128,128]{1,2,0:T(8,128)S(1)} custom-call(f32[1,128,128]{2,1,0:T(8,128)S(1)} %get-tuple-element.54), custom_call_target="InvertDiagBlocksLowerTriangular" | custom-call | tf_op jit(solution)/shard_map/jit(cholesky)/cholesky | solution.py:97
  425.8 1.8 convolution_subtract_fusion.11
  427.6 11.7 %cholesky.564 = f32[128,128]{1,0:T(8,128)S(1)} custom-call(f32[128,128]{1,0:T(8,128)S(1)} %convolution_subtract_fusion.11), custom_call_target="Cholesky" | custom-call | tf_op jit(solution)/shard_map/jit(cholesky)/cholesky | solution.py:97
  446.2 5.0 select_select_fusion
  451.3 24.1 %while.1 = (s32[]{:T(128)}, f32[1024,1024]{1,0:T(8,128)}, s32[8,2]{0,1:T(2,128)S(1)}, f32[8,128,128]{2,1,0:T(8,128)S(1)}, s32[]{:T(128)}) while((s32[]{:T(128)}, f32[1024,1024]{1,0:T(8,128)}, s32[8,2]{0,1:T(2,128)S(1)}, f32[8,128,128]{2,1,0:T(8,128)S(1)}, s32[]{:T(128)}) %tuple.67), condition=%wide.while_cond, body=%wide.while_body.sunk | while | flops 2 | bytes 131181 | solution.py:100
  451.9 2.3 bitcast_dynamic-update-slice_fusion.2
  455.0 2.3 bitcast_dynamic-update-slice_fusion.2
  458.0 2.3 bitcast_dynamic-update-slice_fusion.2
  461.0 2.3 bitcast_dynamic-update-slice_fusion.2
  464.0 2.3 bitcast_dynamic-update-slice_fusion.2
  467.1 2.3 bitcast_dynamic-update-slice_fusion.2
  470.1 2.3 bitcast_dynamic-update-slice_fusion.2
  473.1 2.3 bitcast_dynamic-update-slice_fusion.2
  475.4 79.0 %custom-call.69 = f32[8,128,128]{1,2,0:T(8,128)S(1)} custom-call(f32[8,128,128]{2,1,0:T(8,128)S(1)} %get-tuple-element.9), custom_call_target="InvertDiagBlocksLowerTriangular" | custom-call | tf_op jit(solution)/shard_map/triangular_solve | solution.py:100
  554.4 1.8 convert_add_fusion
  556.9 1.5 convolution_subtract_fusion.4
  559.1 1.6 convolution_subtract_fusion
  561.5 2.1 fusion.15
  564.3 2.2 fusion.18
  567.2 2.7 convolution_subtract_fusion.2
  570.6 3.0 convolution_subtract_fusion.1
  574.3 3.3 convolution_subtract_fusion.3
  578.2 2.0 copy-done.6
  583.4 2.1 multiply_reduce_fusion
  585.4 72.5 %all-gather.8.cloned.1.call-done = f32[2048,1024]{0,1:T(8,128)} async-done(((f32[128,1024]{0,1:T(8,128)}), f32[2048,1024]{0,1:T(8,128)}) %all-gather.8.cloned.1.call-update) | async-done | bytes 8388624 | tf_op jit(solution)/shard_map/all_gather | solution.py:105
  657.9 29.8 %fusion.80 = f32[1024,2048]{1,0:T(8,128)S(1)} fusion(f32[1024,1024]{0,1:T(8,128)} %copy-done.6, f32[2048,1024]{0,1:T(8,128)} %all-gather.8.cloned.1.call-done), kind=kOutput, calls=%fused_computation.212 | convolution fusion | flops 25769803776 | bytes 20971520 | tf_op jit(solution)/shard_map/dot_general | solution.py:29
  687.8 6.1 add_subtract_fusion
  (94 shorter events, 33.3 us)
Async XLA Ops:
  7.2 67.4 %copy-start = (bf16[1024,512]{1,0:T(8,128)(2,1)S(1)}, bf16[1024,512]{1,0:T(8,128)(2,1)}, u32[]{:S(2)}) copy-start(bf16[1024,512]{1,0:T(8,128)(2,1)} %param.3) | copy-start | bytes 3145732
  78.0 24.7 %all-to-all-start = ((bf16[128,4,512]{2,1,0:T(4,128)(2,1)}), bf16[128,4,512]{2,1,0:T(4,128)(2,1)S(1)}, u32[]{:S(2)}, u32[]{:S(2)}) async-start(bf16[128,4,512]{2,1,0:T(4,128)(2,1)} %broadcast_select_fusion.1), calls=%async_computation | async-start | bytes 1048576 | tf_op jit(solution)/shard_map/all_to_all | solution.py:67
  89.2 34.9 %all-gather.4.cloned.1.call-start = ((), (), s32[]{:S(2)}) async-start(), calls=%async_computation.1 | async-start | bytes 1179648 | tf_op jit(solution)/shard_map/all_gather | solution.py:77
  104.6 110.6 %all-reduce.3.cloned.1.call-start = ((), (), s32[]{:S(2)}) async-start(), calls=%async_computation.3 | async-start | bytes 2097152 | tf_op jit(solution)/shard_map/psum | solution.py:14
  125.1 458.3 %all-gather.6.cloned.1.call-start = ((), (), s32[]{:S(2)}) async-start(), calls=%async_computation.2 | async-start | bytes 2228224 | tf_op jit(solution)/shard_map/all_gather | solution.py:78
  125.8 532.1 %all-gather.8.cloned.1.call-start = ((), (), s32[]{:S(2)}) async-start(), calls=%async_computation.4 | async-start | bytes 8912896 | tf_op jit(solution)/shard_map/all_gather | solution.py:105
  241.2 1.9 copy-start.2
  446.2 108.2 %copy-start.3 = (bf16[1024,512]{1,0:T(8,128)(2,1)S(1)}, bf16[1024,512]{1,0:T(8,128)(2,1)}, u32[]{:S(2)}) copy-start(bf16[1024,512]{1,0:T(8,128)(2,1)} %all-reduce.3.cloned.1.call-done) | copy-start | bytes 3145732
  446.2 108.2 %copy-start.4 = (bf16[1024,512]{1,0:T(8,128)(2,1)S(1)}, bf16[1024,512]{1,0:T(8,128)(2,1)}, u32[]{:S(2)}) copy-start(bf16[1024,512]{1,0:T(8,128)(2,1)} %all-gather.4.cloned.1.call-done) | copy-start | bytes 3145732
  578.2 2.0 copy-start.6
  657.9 29.8 %copy-start.5 = (bf16[2048,512]{1,0:T(8,128)(2,1)S(1)}, bf16[2048,512]{1,0:T(8,128)(2,1)}, u32[]{:S(2)}) copy-start(bf16[2048,512]{1,0:T(8,128)(2,1)} %all-gather.6.cloned.1.call-done) | copy-start | bytes 6291460
  687.8 6.1 copy-start.1
Sparse Core Ops, SparseCore 0:
  104.8 19.2 all-gather.3
  127.9 87.3 all-reduce.2
  217.4 44.5 all-gather.5
  581.3 76.5 all-gather.7
where the time goes:
time: 708 us; the launch traced here: 701 us
  other arithmetic  277 us (39%)
  waiting for transfers between devices  193 us (27%)
  local copies, waits for them, and re-layouts  109 us (15%)
  matrix products  90.4 us (13%)
  between operations  20.1 us (3%)
  starting transfers between devices  11.3 us (2%)
    another operation x30, other arithmetic, body(): diag_factor = jnp.linalg.cholesky(diag_block)  172 us
    psum x1, waiting for transfers between devices, broadcast(): return lax.psum(block, axis)  87.8 us
    another operation x3, other arithmetic, body(): lax.linalg.triangular_solve(diag_factor, row_block, left_side=False, lowe...  84 us
    all_gather x1, waiting for transfers between devices, body(): lax.all_gather(own_rows, 'row', axis=0, tiled=True)  72.5 us
    scatter x1, local copies, waits for them, and re-layouts, body(): slot_rows = jnp.zeros((device_count * capacity,), jnp.int32).at[targets.r...  60.3 us
    dot_general x1, matrix products, transposed_product(): lax.dot_general(left, right, (((1,), (1,)), ((), ())), precision=lax.Prec...  29.8 us
    another operation x24, local copies, waits for them, and re-layouts  24 us
    another operation x14, matrix products, body(): diag_factor = jnp.linalg.cholesky(diag_block)  23.2 us
  transfers between devices with their start and end apart: 5, of which 4 were waited for; matrix products, arithmetic and copies ran while one was open for 52% of the time, Pallas kernels for 0%

commit v1 on v0

--- a/solution.py
+++ b/solution.py
@@ -7,6 +7,30 @@
 PANEL = 1024
 GROUP = 128
 ridge = 1.0
+
+
+def read_threads_on_mesh(z, ndim_at):
+    o_now = list(z.shape[1:])
+    o_now[ndim_at] *= z.shape[0]
+    base_arr = jnp.moveaxis(z, 0, ndim_at).reshape(o_now)
+    return base_arr
+
+
+def assign_side_for(unit, axis_name, d_out):
+    world_n = jax.lax.axis_size(axis_name)
+    lanes = tuple(((dev, (dev + 1) % world_n) for dev in range(world_n)))
+    made = tuple(((dev_j, s) for s, dev_j in lanes))
+    all_rows, before = ([], [])
+    for ii in range(world_n - 1):
+        if ii % 2 == 0:
+            all_rows.append(jax.lax.ppermute(all_rows[-1] if all_rows else unit, axis_name, lanes))
+        else:
+            before.append(jax.lax.ppermute(before[-1] if before else unit, axis_name, perm=made))
+    outcome_arr = jnp.stack([*all_rows[::-1], unit, *before], axis=0)
+    tmp = jax.lax.axis_index(axis_name) - len(all_rows)
+    outcome_arr = outcome_arr[(jnp.arange(world_n) - tmp) % world_n]
+    seen_now = read_threads_on_mesh(outcome_arr, d_out)
+    return seen_now
 
 
 def broadcast(block, axis, holder):
@@ -101,9 +125,7 @@
         diag_factor, row_block, left_side=False, lower=True, transpose_a=True
     )
     own_rows = lax.dynamic_slice_in_dim(row_factor, my_col * GROUP, GROUP, 0)
-    schur = tile - transposed_product(
-        row_factor, lax.all_gather(own_rows, "row", axis=0, tiled=True)
-    )
+    schur = tile - transposed_product(row_factor, assign_side_for(own_rows, "row", 0))
     share = PANEL // cols_axis
     panel_factor = lax.dynamic_slice_in_dim(row_factor, my_col * share, share, 1)
     return (schur, panel_factor)

time: 708 us -> 817 us (1.15)
  starting transfers between devices: 11.3 us -> 50.4 us
  local copies, waits for them, and re-layouts: 109 us -> 145 us
  matrix products: 90.4 us -> 117 us
    ppermute x0 -> x15, waiting for transfers between devices: none -> 76.3 us  [the longest x8 74 us: assign_side_for(): jax.lax.ppermute(all_rows[-1] if all_rows else unit, axis_name, lanes)]
    all_gather x1 -> x0, waiting for transfers between devices: 72.5 us -> none  [body(): lax.all_gather(own_rows, 'row', axis=0, tiled=True)]
    ppermute x0 -> x15, starting transfers between devices: none -> 39.2 us  [the longest x7 38 us: assign_side_for(): jax.lax.ppermute(before[-1] if before else unit, axis_name, perm=made)]
    dot_general x1, matrix products: 29.8 us -> 55.8 us  [transposed_product(): lax.dot_general(left, right, (((1,), (1,)), ((), ())), precision=lax.Prec...]
    unnamed x15 -> x50, local copies, waits for them, and re-layouts: 4.95 us -> 24.7 us
    gather x0 -> x2, local copies, waits for them, and re-layouts: none -> 16.9 us  [assign_side_for(): outcome_arr = outcome_arr[(jnp.arange(world_n) - tmp) % world_n]]
    another operation x24 -> x25, local copies, waits for them, and re-layouts: 24 us -> 24.8 us
  transfers between devices with their start and end apart: 5 -> 19, of which waited for: 4 -> 12; matrix products, arithmetic and copies ran while one was open for 52% -> 3% of each run, Pallas kernels for 0% -> 0%
where the time goes in v1:
time: 817 us; the launch traced here: 807 us
  other arithmetic  277 us (34%)
  waiting for transfers between devices  197 us (24%)
  local copies, waits for them, and re-layouts  145 us (18%)
  matrix products  117 us (14%)
  starting transfers between devices  50.4 us (6%)
  between operations  20.2 us (2%)
    another operation x30, other arithmetic, body(): diag_factor = jnp.linalg.cholesky(diag_block)  172 us
    psum x1, waiting for transfers between devices, broadcast(): return lax.psum(block, axis)  88.5 us
    another operation x3, other arithmetic, body(): lax.linalg.triangular_solve(diag_factor, row_block, left_side=False, lowe...  83.8 us
    ppermute x8, waiting for transfers between devices, assign_side_for(): jax.lax.ppermute(all_rows[-1] if all_rows else unit, axis_name, lanes)  74 us
    scatter x1, local copies, waits for them, and re-layouts, body(): slot_rows = jnp.zeros((device_count * capacity,), jnp.int32).at[targets.r...  60.3 us
    dot_general x1, matrix products, transposed_product(): lax.dot_general(left, right, (((1,), (1,)), ((), ())), precision=lax.Prec...  55.8 us
    ppermute x7, starting transfers between devices, assign_side_for(): jax.lax.ppermute(before[-1] if before else unit, axis_name, perm=made)  38 us
    unnamed x50, local copies, waits for them, and re-layouts  24.7 us
  transfers between devices with their start and end apart: 19, of which 12 were waited for; matrix products, arithmetic and copies ran while one was open for 3% of the time, Pallas kernels for 0%

profile of v1, /device:TPU:0, one launch (start us, length us, event | category | flops | bytes accessed | tf_op | source)
XLA Modules:
  0.0 806.6 jit_solution(7102787759243249244)
XLA Ops:
  8.2 5.1 convert_reduce_fusion
  14.3 60.3 %scatter_custom_fusion = s32[512]{0:T(512)S(1)} fusion(s32[16384]{0:T(1024)S(1)} %get-tuple-element.74, s32[16384]{0:T(1024)S(1)} %get-tuple-element.73, s32[]{:T(128)} %copy.100), kind=kCustom, calls=%fused_computation.219 | custom fusion | bytes 2052 | tf_op jit(solution)/shard_map/scatter | solution.py:88
  78.0 11.2 %all-to-all-start = ((bf16[128,4,512]{2,1,0:T(4,128)(2,1)}), bf16[128,4,512]{2,1,0:T(4,128)(2,1)S(1)}, u32[]{:S(2)}, u32[]{:S(2)}) async-start(bf16[128,4,512]{2,1,0:T(4,128)(2,1)} %broadcast_select_fusion.1), calls=%async_computation | async-start | bytes 1048576 | tf_op jit(solution)/shard_map/all_to_all | solution.py:91
  89.2 13.4 %all-to-all-done = bf16[128,4,512]{2,1,0:T(4,128)(2,1)S(1)} async-done(((bf16[128,4,512]{2,1,0:T(4,128)(2,1)}), bf16[128,4,512]{2,1,0:T(4,128)(2,1)S(1)}, u32[]{:S(2)}, u32[]{:S(2)}) %all-to-all-start) | async-done | bytes 524320 | tf_op jit(solution)/shard_map/all_to_all | solution.py:91
  105.4 18.7 %all-gather.3.cloned.1.call-done = bf16[1024,512]{1,0:T(8,128)(2,1)} async-done(((bf16[128,512]{1,0:T(8,128)(2,1)}), bf16[1024,512]{1,0:T(8,128)(2,1)}) %all-gather.3.cloned.1.call-update) | async-done | bytes 1048592 | tf_op jit(solution)/shard_map/all_gather | solution.py:101
  126.7 88.5 %all-reduce.3.cloned.1.call-done = bf16[1024,512]{1,0:T(8,128)(2,1)} async-done(((bf16[1024,512]{1,0:T(8,128)(2,1)}), bf16[1024,512]{1,0:T(8,128)(2,1)}) %all-reduce.3.cloned.1.call-update) | async-done | bytes 1048592 | tf_op jit(solution)/shard_map/psum | solution.py:38
  216.7 7.7 broadcast_add_fusion
  224.4 5.3 copy.21
  229.7 5.3 copy.22
  235.0 6.3 add_multiply_fusion
  243.3 11.7 %cholesky.223 = f32[128,128]{1,0:T(8,128)S(1)} custom-call(f32[128,128]{1,0:T(8,128)S(1)} %cholesky.580), custom_call_target="Cholesky" | custom-call | tf_op jit(solution)/shard_map/jit(cholesky)/cholesky | solution.py:121
  255.0 2.5 cholesky.255
  257.6 9.8 %custom-call.62 = f32[1,128,128]{1,2,0:T(8,128)S(1)} custom-call(f32[1,128,128]{2,1,0:T(8,128)S(1)} %get-tuple-element.72), custom_call_target="InvertDiagBlocksLowerTriangular" | custom-call | tf_op jit(solution)/shard_map/jit(cholesky)/cholesky | solution.py:121
  267.4 2.3 constant_dynamic-update-slice_fusion.25
  271.2 11.7 %cholesky.244 = f32[128,128]{1,0:T(8,128)S(1)} custom-call(f32[128,128]{1,0:T(8,128)S(1)} %cholesky.584), custom_call_target="Cholesky" | custom-call | tf_op jit(solution)/shard_map/jit(cholesky)/cholesky | solution.py:121
  283.6 9.9 %custom-call.63 = f32[1,128,128]{1,2,0:T(8,128)S(1)} custom-call(f32[1,128,128]{2,1,0:T(8,128)S(1)} %get-tuple-element.69), custom_call_target="InvertDiagBlocksLowerTriangular" | custom-call | tf_op jit(solution)/shard_map/jit(cholesky)/cholesky | solution.py:121
  296.9 11.7 %cholesky.468 = f32[128,128]{1,0:T(8,128)S(1)} custom-call(f32[128,128]{1,0:T(8,128)S(1)} %cholesky.589), custom_call_target="Cholesky" | custom-call | tf_op jit(solution)/shard_map/jit(cholesky)/cholesky | solution.py:121
  309.9 9.8 %custom-call.64 = f32[1,128,128]{1,2,0:T(8,128)S(1)} custom-call(f32[1,128,128]{2,1,0:T(8,128)S(1)} %get-tuple-element.66), custom_call_target="InvertDiagBlocksLowerTriangular" | custom-call | tf_op jit(solution)/shard_map/jit(cholesky)/cholesky | solution.py:121
  320.8 2.3 convolution_subtract_fusion.7
  323.2 11.9 %cholesky.487 = f32[128,128]{1,0:T(8,128)S(1)} custom-call(f32[128,128]{1,0:T(8,128)S(1)} %cholesky.594), custom_call_target="Cholesky" | custom-call | tf_op jit(solution)/shard_map/jit(cholesky)/cholesky | solution.py:121
  336.4 9.8 %custom-call.65 = f32[1,128,128]{1,2,0:T(8,128)S(1)} custom-call(f32[1,128,128]{2,1,0:T(8,128)S(1)} %get-tuple-element.63), custom_call_target="InvertDiagBlocksLowerTriangular" | custom-call | tf_op jit(solution)/shard_map/jit(cholesky)/cholesky | solution.py:121
  347.3 2.3 convolution_subtract_fusion.8
  349.6 11.7 %cholesky.506 = f32[128,128]{1,0:T(8,128)S(1)} custom-call(f32[128,128]{1,0:T(8,128)S(1)} %cholesky.599), custom_call_target="Cholesky" | custom-call | tf_op jit(solution)/shard_map/jit(cholesky)/cholesky | solution.py:121
  362.7 9.8 %custom-call.66 = f32[1,128,128]{1,2,0:T(8,128)S(1)} custom-call(f32[1,128,128]{2,1,0:T(8,128)S(1)} %get-tuple-element.60), custom_call_target="InvertDiagBlocksLowerTriangular" | custom-call | tf_op jit(solution)/shard_map/jit(cholesky)/cholesky | solution.py:121
  373.5 2.7 convolution_subtract_fusion.9
  376.2 11.7 %cholesky.526 = f32[128,128]{1,0:T(8,128)S(1)} custom-call(f32[128,128]{1,0:T(8,128)S(1)} %cholesky.604), custom_call_target="Cholesky" | custom-call | tf_op jit(solution)/shard_map/jit(cholesky)/cholesky | solution.py:121
  389.2 9.8 %custom-call.67 = f32[1,128,128]{1,2,0:T(8,128)S(1)} custom-call(f32[1,128,128]{2,1,0:T(8,128)S(1)} %get-tuple-element.57), custom_call_target="InvertDiagBlocksLowerTriangular" | custom-call | tf_op jit(solution)/shard_map/jit(cholesky)/cholesky | solution.py:121
  402.1 11.7 %cholesky.546 = f32[128,128]{1,0:T(8,128)S(1)} custom-call(f32[128,128]{1,0:T(8,128)S(1)} %cholesky.609), custom_call_target="Cholesky" | custom-call | tf_op jit(solution)/shard_map/jit(cholesky)/cholesky | solution.py:121
  415.1 10.0 %custom-call.68 = f32[1,128,128]{1,2,0:T(8,128)S(1)} custom-call(f32[1,128,128]{2,1,0:T(8,128)S(1)} %get-tuple-element.54), custom_call_target="InvertDiagBlocksLowerTriangular" | custom-call | tf_op jit(solution)/shard_map/jit(cholesky)/cholesky | solution.py:121
  427.7 11.7 %cholesky.564 = f32[128,128]{1,0:T(8,128)S(1)} custom-call(f32[128,128]{1,0:T(8,128)S(1)} %convolution_subtract_fusion.11), custom_call_target="Cholesky" | custom-call | tf_op jit(solution)/shard_map/jit(cholesky)/cholesky | solution.py:121
  446.3 5.0 select_select_fusion
  451.4 24.1 %while.1 = (s32[]{:T(128)}, f32[1024,1024]{1,0:T(8,128)}, s32[8,2]{0,1:T(2,128)S(1)}, f32[8,128,128]{2,1,0:T(8,128)S(1)}, s32[]{:T(128)}) while((s32[]{:T(128)}, f32[1024,1024]{1,0:T(8,128)}, s32[8,2]{0,1:T(2,128)S(1)}, f32[8,128,128]{2,1,0:T(8,128)S(1)}, s32[]{:T(128)}) %tuple.67), condition=%wide.while_cond, body=%wide.while_body.sunk | while | flops 2 | bytes 131181 | solution.py:124
  452.0 2.3 bitcast_dynamic-update-slice_fusion.18
  455.1 2.3 bitcast_dynamic-update-slice_fusion.18
  458.1 2.3 bitcast_dynamic-update-slice_fusion.18
  461.1 2.3 bitcast_dynamic-update-slice_fusion.18
  464.2 2.3 bitcast_dynamic-update-slice_fusion.18
  467.2 2.3 bitcast_dynamic-update-slice_fusion.18
  470.2 2.3 bitcast_dynamic-update-slice_fusion.18
  473.2 2.3 bitcast_dynamic-update-slice_fusion.18
  475.5 78.8 %custom-call.69 = f32[8,128,128]{1,2,0:T(8,128)S(1)} custom-call(f32[8,128,128]{2,1,0:T(8,128)S(1)} %get-tuple-element.9), custom_call_target="InvertDiagBlocksLowerTriangular" | custom-call | tf_op jit(solution)/shard_map/triangular_solve | solution.py:124
  567.2 2.7 convolution_subtract_fusion.2
  570.6 3.3 convolution_subtract_fusion.1
  574.5 3.3 convolution_subtract_fusion.3
  581.7 14.5 %collective-permute-done = f32[128,1024]{0,1:T(8,128)S(1)} collective-permute-done((f32[128,1024]{0,1:T(8,128)S(1)}, f32[128,1024]{0,1:T(8,128)S(1)}, u32[]{:S(2)}, u32[]{:S(2)}) %collective-permute-start) | collective-permute-done | bytes 524320 | tf_op jit(solution)/shard_map/ppermute | solution.py:26
  596.2 5.3 collective-permute-start.8
  601.5 10.8 %collective-permute-done.1 = f32[128,1024]{0,1:T(8,128)S(1)} collective-permute-done((f32[128,1024]{0,1:T(8,128)S(1)}, f32[128,1024]{0,1:T(8,128)S(1)}, u32[]{:S(2)}, u32[]{:S(2)}) %collective-permute-start.1) | collective-permute-done | bytes 524320 | tf_op jit(solution)/shard_map/ppermute | solution.py:26
  612.4 5.3 collective-permute-start.9
  617.7 10.7 %collective-permute-done.2 = f32[128,1024]{0,1:T(8,128)S(1)} collective-permute-done((f32[128,1024]{0,1:T(8,128)S(1)}, f32[128,1024]{0,1:T(8,128)S(1)}, u32[]{:S(2)}, u32[]{:S(2)}) %collective-permute-start.2) | collective-permute-done | bytes 524320 | tf_op jit(solution)/shard_map/ppermute | solution.py:26
  628.4 2.2 collective-permute-done.9
  630.6 5.8 collective-permute-start.10
  636.4 10.3 %collective-permute-done.3 = f32[128,1024]{0,1:T(8,128)S(1)} collective-permute-done((f32[128,1024]{0,1:T(8,128)S(1)}, f32[128,1024]{0,1:T(8,128)S(1)}, u32[]{:S(2)}, u32[]{:S(2)}) %collective-permute-start.3) | collective-permute-done | bytes 524320 | tf_op jit(solution)/shard_map/ppermute | solution.py:26
  646.8 5.4 collective-permute-start.11
  652.2 8.9 %collective-permute-done.4 = f32[128,1024]{0,1:T(8,128)S(1)} collective-permute-done((f32[128,1024]{0,1:T(8,128)S(1)}, f32[128,1024]{0,1:T(8,128)S(1)}, u32[]{:S(2)}, u32[]{:S(2)}) %collective-permute-start.4) | collective-permute-done | bytes 524320 | tf_op jit(solution)/shard_map/ppermute | solution.py:26
  661.1 5.3 collective-permute-start.12
  666.4 8.2 %collective-permute-done.5 = f32[128,1024]{0,1:T(8,128)} collective-permute-done((f32[128,1024]{0,1:T(8,128)S(1)}, f32[128,1024]{0,1:T(8,128)}, u32[]{:S(2)}, u32[]{:S(2)}) %collective-permute-start.5) | collective-permute-done | bytes 524320 | tf_op jit(solution)/shard_map/ppermute | solution.py:26
  674.8 5.4 collective-permute-start.13
  680.1 7.5 collective-permute-done.6
  692.0 5.4 collective-permute-start.14
  697.4 3.1 collective-permute-done.7
  721.0 7.7 gather_fusion.2
  728.7 9.2 %copy.30 = f32[16,128,1024]{2,1,0:T(8,128)} copy(f32[16,128,1024]{1,2,0:T(8,128)} %gather_fusion.2) | data formatting | bytes 16777216 | tf_op jit(solution)/shard_map/gather | solution.py:31
  738.0 55.8 %fusion.82 = f32[1024,2048]{1,0:T(8,128)S(1)} fusion(f32[1024,1024]{0,1:T(8,128)} %copy-done.6, f32[2048,1024]{1,0:T(8,128)} %bitcast.181), kind=kOutput, calls=%fused_computation.236 | convolution fusion | flops 25769803776 | bytes 20971520 | tf_op jit(solution)/shard_map/dot_general | solution.py:53
  793.8 6.1 add_subtract_fusion
  (161 shorter events, 84.6 us)
Async XLA Ops:
  7.2 67.4 %copy-start = (bf16[1024,512]{1,0:T(8,128)(2,1)S(1)}, bf16[1024,512]{1,0:T(8,128)(2,1)}, u32[]{:S(2)}) copy-start(bf16[1024,512]{1,0:T(8,128)(2,1)} %param.3) | copy-start | bytes 3145732
  78.0 24.7 %all-to-all-start = ((bf16[128,4,512]{2,1,0:T(4,128)(2,1)}), bf16[128,4,512]{2,1,0:T(4,128)(2,1)S(1)}, u32[]{:S(2)}, u32[]{:S(2)}) async-start(bf16[128,4,512]{2,1,0:T(4,128)(2,1)} %broadcast_select_fusion.1), calls=%async_computation | async-start | bytes 1048576 | tf_op jit(solution)/shard_map/all_to_all | solution.py:91
  89.2 34.9 %all-gather.3.cloned.1.call-start = ((), (), s32[]{:S(2)}) async-start(), calls=%async_computation.1 | async-start | bytes 1179648 | tf_op jit(solution)/shard_map/all_gather | solution.py:101
  104.6 110.6 %all-reduce.3.cloned.1.call-start = ((), (), s32[]{:S(2)}) async-start(), calls=%async_computation.3 | async-start | bytes 2097152 | tf_op jit(solution)/shard_map/psum | solution.py:38
  125.1 564.7 %all-gather.5.cloned.1.call-start = ((), (), s32[]{:S(2)}) async-start(), calls=%async_computation.2 | async-start | bytes 2228224 | tf_op jit(solution)/shard_map/all_gather | solution.py:102
  241.3 1.9 copy-start.2
  446.3 108.0 %copy-start.3 = (bf16[1024,512]{1,0:T(8,128)(2,1)S(1)}, bf16[1024,512]{1,0:T(8,128)(2,1)}, u32[]{:S(2)}) copy-start(bf16[1024,512]{1,0:T(8,128)(2,1)} %all-reduce.3.cloned.1.call-done) | copy-start | bytes 3145732
  446.3 108.0 %copy-start.4 = (bf16[1024,512]{1,0:T(8,128)(2,1)S(1)}, bf16[1024,512]{1,0:T(8,128)(2,1)}, u32[]{:S(2)}) copy-start(bf16[1024,512]{1,0:T(8,128)(2,1)} %all-gather.3.cloned.1.call-done) | copy-start | bytes 3145732
  578.5 2.0 copy-start.6
  580.5 15.7 %collective-permute-start = (f32[128,1024]{0,1:T(8,128)S(1)}, f32[128,1024]{0,1:T(8,128)S(1)}, u32[]{:S(2)}, u32[]{:S(2)}) collective-permute-start(f32[128,1024]{0,1:T(8,128)S(1)} %constant_dynamic-slice_fusion.2), channel_id=1, source_target_pairs={{0,8},{8,16},{16,24},{24,32},{32,40},{40,48},{48,56},{56,64},{64,7... | collective-permute-start | bytes 1572872 | tf_op jit(solution)/shard_map/ppermute | solution.py:26
  596.2 16.2 %collective-permute-start.1 = (f32[128,1024]{0,1:T(8,128)S(1)}, f32[128,1024]{0,1:T(8,128)S(1)}, u32[]{:S(2)}, u32[]{:S(2)}) collective-permute-start(f32[128,1024]{0,1:T(8,128)S(1)} %collective-permute-done), channel_id=1, source_target_pairs={{0,8},{8,16},{16,24},{24,32},{32,40},{40,48},{48,56},{56,64},{64,7... | collective-permute-start | bytes 1572872 | tf_op jit(solution)/shard_map/ppermute | solution.py:26
  596.2 16.2 %collective-permute-start.8 = (f32[128,1024]{0,1:T(8,128)S(1)}, f32[128,1024]{0,1:T(8,128)S(1)}, u32[]{:S(2)}, u32[]{:S(2)}) collective-permute-start(f32[128,1024]{0,1:T(8,128)S(1)} %constant_dynamic-slice_fusion.2), channel_id=1, source_target_pairs={{8,0},{16,8},{24,16},{32,24},{40,32},{48,40},{56,48},{64,56},{72,6... | collective-permute-start | bytes 1572872 | tf_op jit(solution)/shard_map/ppermute | solution.py:28
  612.4 16.0 %collective-permute-start.2 = (f32[128,1024]{0,1:T(8,128)S(1)}, f32[128,1024]{0,1:T(8,128)S(1)}, u32[]{:S(2)}, u32[]{:S(2)}) collective-permute-start(f32[128,1024]{0,1:T(8,128)S(1)} %collective-permute-done.1), channel_id=1, source_target_pairs={{0,8},{8,16},{16,24},{24,32},{32,40},{40,48},{48,56},{56,64},{64,7... | collective-permute-start | bytes 1572872 | tf_op jit(solution)/shard_map/ppermute | solution.py:26
  612.4 18.2 %collective-permute-start.9 = (f32[128,1024]{0,1:T(8,128)S(1)}, f32[128,1024]{0,1:T(8,128)S(1)}, u32[]{:S(2)}, u32[]{:S(2)}) collective-permute-start(f32[128,1024]{0,1:T(8,128)S(1)} %collective-permute-done.8), channel_id=1, source_target_pairs={{8,0},{16,8},{24,16},{32,24},{40,32},{48,40},{56,48},{64,56},{72,6... | collective-permute-start | bytes 1572872 | tf_op jit(solution)/shard_map/ppermute | solution.py:28
  628.4 18.4 %copy-start.9 = (f32[128,1024]{0,1:T(8,128)}, f32[128,1024]{0,1:T(8,128)S(1)}, u32[]{:S(2)}) copy-start(f32[128,1024]{0,1:T(8,128)S(1)} %collective-permute-done.2) | copy-start | bytes 1572868
  628.4 18.4 %collective-permute-start.3 = (f32[128,1024]{0,1:T(8,128)S(1)}, f32[128,1024]{0,1:T(8,128)S(1)}, u32[]{:S(2)}, u32[]{:S(2)}) collective-permute-start(f32[128,1024]{0,1:T(8,128)S(1)} %collective-permute-done.2), channel_id=1, source_target_pairs={{0,8},{8,16},{16,24},{24,32},{32,40},{40,48},{48,56},{56,64},{64,7... | collective-permute-start | bytes 1572872 | tf_op jit(solution)/shard_map/ppermute | solution.py:26
  630.6 57.0 %copy-start.7 = (f32[128,1024]{0,1:T(8,128)}, f32[128,1024]{0,1:T(8,128)S(1)}, u32[]{:S(2)}) copy-start(f32[128,1024]{0,1:T(8,128)S(1)} %collective-permute-done.9) | copy-start | bytes 1572868
  630.6 16.1 %collective-permute-start.10 = (f32[128,1024]{0,1:T(8,128)S(1)}, f32[128,1024]{0,1:T(8,128)S(1)}, u32[]{:S(2)}, u32[]{:S(2)}) collective-permute-start(f32[128,1024]{0,1:T(8,128)S(1)} %collective-permute-done.9), channel_id=1, source_target_pairs={{8,0},{16,8},{24,16},{32,24},{40,32},{48,40},{56,48},{64,56},{72,6... | collective-permute-start | bytes 1572872 | tf_op jit(solution)/shard_map/ppermute | solution.py:28
  646.7 14.4 %copy-start.13 = (f32[128,1024]{0,1:T(8,128)}, f32[128,1024]{0,1:T(8,128)S(1)}, u32[]{:S(2)}) copy-start(f32[128,1024]{0,1:T(8,128)S(1)} %collective-permute-done.3) | copy-start | bytes 1572868
  646.7 14.3 %collective-permute-start.4 = (f32[128,1024]{0,1:T(8,128)S(1)}, f32[128,1024]{0,1:T(8,128)S(1)}, u32[]{:S(2)}, u32[]{:S(2)}) collective-permute-start(f32[128,1024]{0,1:T(8,128)S(1)} %collective-permute-done.3), channel_id=1, source_target_pairs={{0,8},{8,16},{16,24},{24,32},{32,40},{40,48},{48,56},{56,64},{64,7... | collective-permute-start | bytes 1572872 | tf_op jit(solution)/shard_map/ppermute | solution.py:26
  646.8 5.4 copy-start.11
  646.8 14.3 %collective-permute-start.11 = (f32[128,1024]{0,1:T(8,128)S(1)}, f32[128,1024]{0,1:T(8,128)}, u32[]{:S(2)}, u32[]{:S(2)}) collective-permute-start(f32[128,1024]{0,1:T(8,128)S(1)} %collective-permute-done.10), channel_id=1, source_target_pairs={{8,0},{16,8},{24,16},{32,24},{40,32},{48,40},{56,48},{64,56},{72,6... | collective-permute-start | bytes 1572872 | tf_op jit(solution)/shard_map/ppermute | solution.py:28
  661.1 5.4 copy-start.15
  661.1 13.6 %collective-permute-start.5 = (f32[128,1024]{0,1:T(8,128)S(1)}, f32[128,1024]{0,1:T(8,128)}, u32[]{:S(2)}, u32[]{:S(2)}) collective-permute-start(f32[128,1024]{0,1:T(8,128)S(1)} %collective-permute-done.4), channel_id=1, source_target_pairs={{0,8},{8,16},{16,24},{24,32},{32,40},{40,48},{48,56},{56,64},{64,7... | collective-permute-start | bytes 1572872 | tf_op jit(solution)/shard_map/ppermute | solution.py:26
  661.1 13.7 %collective-permute-start.12 = (f32[128,1024]{0,1:T(8,128)}, f32[128,1024]{0,1:T(8,128)}, u32[]{:S(2)}, u32[]{:S(2)}) collective-permute-start(f32[128,1024]{0,1:T(8,128)} %collective-permute-done.11), channel_id=1, source_target_pairs={{8,0},{16,8},{24,16},{32,24},{40,32},{48,40},{56,48},{64,56},{72,6... | collective-permute-start | bytes 1572872 | tf_op jit(solution)/shard_map/ppermute | solution.py:28
  674.7 12.9 %collective-permute-start.6 = (f32[128,1024]{0,1:T(8,128)}, f32[128,1024]{0,1:T(8,128)}, u32[]{:S(2)}, u32[]{:S(2)}) collective-permute-start(f32[128,1024]{0,1:T(8,128)} %collective-permute-done.5), channel_id=1, source_target_pairs={{0,8},{8,16},{16,24},{24,32},{32,40},{40,48},{48,56},{56,64},{64,7... | collective-permute-start | bytes 1572872 | tf_op jit(solution)/shard_map/ppermute | solution.py:26
  674.8 17.2 %collective-permute-start.13 = (f32[128,1024]{0,1:T(8,128)}, f32[128,1024]{0,1:T(8,128)}, u32[]{:S(2)}, u32[]{:S(2)}) collective-permute-start(f32[128,1024]{0,1:T(8,128)} %collective-permute-done.12), channel_id=1, source_target_pairs={{8,0},{16,8},{24,16},{32,24},{40,32},{48,40},{56,48},{64,56},{72,6... | collective-permute-start | bytes 1572872 | tf_op jit(solution)/shard_map/ppermute | solution.py:28
  687.6 12.8 %collective-permute-start.7 = (f32[128,1024]{0,1:T(8,128)}, f32[128,1024]{0,1:T(8,128)}, u32[]{:S(2)}, u32[]{:S(2)}) collective-permute-start(f32[128,1024]{0,1:T(8,128)} %collective-permute-done.6), channel_id=1, source_target_pairs={{0,8},{8,16},{16,24},{24,32},{32,40},{40,48},{48,56},{56,64},{64,7... | collective-permute-start | bytes 1572872 | tf_op jit(solution)/shard_map/ppermute | solution.py:26
  689.8 16.3 %copy-start.16 = (f32[128,1024]{0,1:T(8,128)S(1)}, f32[128,1024]{0,1:T(8,128)}, u32[]{:S(2)}) copy-start(f32[128,1024]{0,1:T(8,128)} %copy-done.15) | copy-start | bytes 1572868
  689.8 17.2 %copy-start.14 = (f32[128,1024]{0,1:T(8,128)S(1)}, f32[128,1024]{0,1:T(8,128)}, u32[]{:S(2)}) copy-start(f32[128,1024]{0,1:T(8,128)} %copy-done.13) | copy-start | bytes 1572868
  689.8 18.0 %copy-start.10 = (f32[128,1024]{0,1:T(8,128)S(1)}, f32[128,1024]{0,1:T(8,128)}, u32[]{:S(2)}) copy-start(f32[128,1024]{0,1:T(8,128)} %copy-done.9) | copy-start | bytes 1572868
  692.0 28.2 %collective-permute-start.14 = (f32[128,1024]{0,1:T(8,128)}, f32[128,1024]{0,1:T(8,128)S(1)}, u32[]{:S(2)}, u32[]{:S(2)}) collective-permute-start(f32[128,1024]{0,1:T(8,128)} %collective-permute-done.13), channel_id=1, source_target_pairs={{8,0},{16,8},{24,16},{32,24},{40,32},{48,40},{56,48},{64,56},{72,6... | collective-permute-start | bytes 1572872 | tf_op jit(solution)/shard_map/ppermute | solution.py:28
  704.2 8.8 %copy-start.8 = (f32[128,1024]{0,1:T(8,128)S(1)}, f32[128,1024]{0,1:T(8,128)}, u32[]{:S(2)}) copy-start(f32[128,1024]{0,1:T(8,128)} %copy-done.7) | copy-start | bytes 1572868
  706.1 7.7 copy-start.12
  738.0 55.8 %copy-start.5 = (bf16[2048,512]{1,0:T(8,128)(2,1)S(1)}, bf16[2048,512]{1,0:T(8,128)(2,1)}, u32[]{:S(2)}) copy-start(bf16[2048,512]{1,0:T(8,128)(2,1)} %all-gather.5.cloned.1.call-done) | copy-start | bytes 6291460
  793.8 6.1 copy-start.1
Sparse Core Ops, SparseCore 0:
  104.8 19.2 all-gather.2
  127.9 87.3 all-reduce.2
  581.8 61.4 all-gather.4
